TPU v7x, 32 devices: a whole 2x2x4 slice. The times are simulated.
32 devices in a mesh: dp: 8 (over z, y), phase: 2 (over core), mp: 2 (over x).
Axes of the slice: x: 2, y: 2, z: 4, core: 2. Of those that a mesh axis runs over, the one named last changes fastest.
Arguments:
- sec_acts: bfloat16 [2, 8, 512, 4096], P('phase', 'dp', None, 'mp'), may hold values from -40 to 40
- gain: bfloat16 [4096], P('mp'), may hold values from 0.5 to 1.5
- w_kv: bfloat16 [4096, 4096], P(('dp', 'phase'), 'mp'), may hold values from -0.09375 to 0.09375
- src_len: int32 [8], P('dp'), may hold values from 1 to 512, 2560 in all
- tgt_len: int32 [8], P('dp'), may hold values from 1 to 512, 3072 in all
Outputs:
- sec_grads: bfloat16 [2, 8, 512, 4096], P('phase', 'dp', None, 'mp')
- d_wkv: float32 [4096, 4096], P(('dp', 'phase'), 'mp')
- d_gain: float32 [4096], P('mp')
Inputs may be any that keep to these rules, and one draw needn't show every extreme that they name: Source positions 0 to src_len - 1 of a pair are real, the rest padding; some pair has exactly 512. Target positions 0 to tgt_len - 1 of a pair carry loss, the rest padding; some pair has exactly 512.
All inputs are finite; a program needn't handle non-finite values. No bound on the sum of `src_len` or of `tgt_len` on one device may be relied on, other than what follows from the above.
Results may differ from a plain program's by a relative error of at most 0.022.
Values may be sent and summed in bfloat16 or wider, within the bound.
No kernel may reach another device: no remote copies, remote signals or barrier semaphores. Data moves between devices by JAX's collectives and lax.ppermute only.
A program may use at most 128 MiB of HBM per device.

v0:
```python
import jax
import jax.numpy as jnp
from jax import lax
from jax.sharding import PartitionSpec as P

D = 4096
HEAD = 64
norm_epsilon = 1e-06


def shifted(value, axis, steps):
    count = lax.axis_size(axis)
    initial, last = (max(0, -steps), min(count, count - steps))
    return lax.ppermute(value, axis, [(source, source + steps) for source in range(initial, last)])


def attend_back(queries, grad_out, key_heads, values, key_mask):
    f32 = jnp.float32
    bf16 = jnp.bfloat16
    factor = 1.0 / HEAD**0.5
    scores = factor * jnp.einsum("pihd,pjhd->phij", queries, key_heads, preferred_element_type=f32)
    scores = jnp.where(key_mask[:, None, None, :], scores, -1e30)
    row_top = jnp.max(scores, axis=-1, keepdims=True)
    weights = jnp.exp(scores - row_top)
    probability = weights / jnp.sum(weights, axis=-1, keepdims=True)
    prob_low = probability.astype(bf16)
    attended = jnp.einsum("phij,pjhd->pihd", prob_low, values, preferred_element_type=f32)
    grad_prob = jnp.einsum("pihd,pjhd->phij", grad_out, values, preferred_element_type=f32)
    row_delta = jnp.einsum("pihd,pihd->phi", grad_out.astype(f32), attended)
    grad_score = (factor * probability * (grad_prob - row_delta[..., None])).astype(bf16)
    grad_query = jnp.einsum(
        "phij,pjhd->pihd", grad_score, key_heads, preferred_element_type=f32
    ).astype(bf16)
    grad_key = jnp.einsum(
        "phij,pihd->pjhd", grad_score, queries, preferred_element_type=f32
    ).astype(bf16)
    grad_value = jnp.einsum(
        "phij,pihd->pjhd", prob_low, grad_out, preferred_element_type=f32
    ).astype(bf16)
    return (grad_query, grad_key, grad_value)


def on_device(sec_acts, gain, w_kv, src_len, tgt_len):
    f32 = jnp.float32
    bf16 = jnp.bfloat16
    section = lax.axis_index("phase")
    packed = sec_acts[0]
    pair_dev, length, shard_width = packed.shape
    row_count = pair_dev * length
    pair_total = pair_dev * lax.axis_size("dp")
    pair_scale = 1.0 / pair_total
    hidden = packed.astype(f32)
    squares = lax.psum(jnp.sum(hidden * hidden, axis=-1), "mp")
    inv_rms = lax.rsqrt(squares / D + norm_epsilon)[..., None]
    normed = hidden * inv_rms
    gain_wide = gain.astype(f32)
    enc_shard = (normed * gain_wide).astype(bf16)
    enc_moved = shifted(enc_shard, "phase", 1)
    enc_full = lax.all_gather(enc_moved, "mp", axis=2, tiled=True)
    enc_rows = enc_full.reshape(row_count, D)
    whole_weight = lax.all_gather(w_kv, ("dp", "phase"), axis=0, tiled=True)
    key_value = jnp.dot(enc_rows, whole_weight, preferred_element_type=f32)
    heads_dev = shard_width // (2 * HEAD)
    kv_split = key_value.astype(bf16).reshape(pair_dev, length, heads_dev, 2, HEAD)
    dec_split = packed.reshape(pair_dev, length, heads_dev, 2, HEAD)
    positions = jnp.arange(length, dtype=jnp.int32)
    query_mask = positions[None, :] < tgt_len[:, None]
    key_mask = positions[None, :] < src_len[:, None]
    grad_out = jnp.where(query_mask[:, :, None, None], dec_split[:, :, :, 1], jnp.zeros((), bf16))
    grad_query, grad_key, grad_value = attend_back(
        dec_split[:, :, :, 0], grad_out, kv_split[:, :, :, 0], kv_split[:, :, :, 1], key_mask
    )
    dec_grads = jnp.stack([grad_query, grad_key], axis=3).reshape(pair_dev, length, shard_width)
    grad_kv = jnp.stack([grad_key, grad_value], axis=3).reshape(row_count, shard_width)
    reduced = lax.psum_scatter(
        (
            pair_scale
            * lax.dot_general(
                enc_rows, grad_kv, (((0,), (0,)), ((), ())), preferred_element_type=f32
            )
        ).astype(jnp.bfloat16),
        "dp",
        scatter_dimension=0,
        tiled=True,
    ).astype(jnp.float32)
    half_rows = reduced.shape[0] // 2
    lower_rows = shifted(reduced[:half_rows], "phase", -1)
    d_wkv = jnp.where(section == 0, lower_rows, reduced[half_rows:])
    partial_enc = lax.dot_general(
        grad_kv, whole_weight, (((1,), (1,)), ((), ())), preferred_element_type=f32
    ).astype(bf16)
    partial_enc = partial_enc.reshape(1, pair_dev, length, D)
    pieces = lax.all_to_all(partial_enc, "mp", split_axis=3, concat_axis=0, tiled=True)
    summed = jnp.sum(pieces.astype(f32), axis=0)
    grad_enc = shifted(summed, "phase", -1)
    grad_normed = grad_enc * gain_wide
    gain_term = pair_scale * jnp.sum(grad_enc * normed, axis=(0, 1))
    d_gain = lax.psum(gain_term, ("dp", "phase"))
    sec_grads = jnp.where(section == 0, grad_normed.astype(bf16), dec_grads)[None]
    return (sec_grads, d_wkv, d_gain)


def solution(mesh):
    placed = (P("phase", "dp", None, "mp"), P("mp"), P(("dp", "phase"), "mp"), P("dp"), P("dp"))
    return jax.shard_map(
        on_device,
        mesh=mesh,
        in_specs=placed,
        out_specs=(P("phase", "dp", None, "mp"), P(("dp", "phase"), "mp"), P("mp")),
        check_vma=False,
    )
```

profile of v0, /device:TPU:0, one launch (start us, length us, event | category | flops | bytes accessed | tf_op | source)
XLA Modules:
  0.0 626.1 jit_solution(5916800260280279327)
XLA Ops:
  7.2 0.0 all-gather.3.cloned.1.call-start
  7.2 0.7 convert_element_type.108
  7.9 2.1 fusion.14
  10.0 0.0 copy-start
  10.0 6.0 psum.14
  16.0 2.1 fusion.12
  18.1 2.7 collective-permute-start
  20.8 2.5 collective-permute-done
  23.3 0.0 all-gather.3.cloned.1.call-update
  23.3 0.0 all-gather.5.cloned.1.call-start
  23.4 0.7 all-gather.5.cloned.1.call-update
  24.1 0.0 reduce-scatter.2.cloned.1.call-start
  24.1 0.0 copy-done
  24.1 2.5 copy.33
  28.0 54.1 %all-gather.3.cloned.1.call-done = bf16[1,512,4096]{2,1,0:T(8,128)(2,1)} async-done(((bf16[1,512,2048]{2,1,0:T(8,128)(2,1)}), bf16[1,512,4096]{2,1,0:T(8,128)(2,1)}) %all-gather.3.cloned.1.call-update) | async-done | bytes 4194320 | tf_op jit(solution)/shard_map/all_gather | solution.py:59
  82.1 129.1 %all-gather.5.cloned.1.call-done = bf16[4096,2048]{1,0:T(8,128)(2,1)} async-done(((bf16[256,2048]{1,0:T(8,128)(2,1)}), bf16[4096,2048]{1,0:T(8,128)(2,1)}) %all-gather.5.cloned.1.call-update) | async-done | bytes 16777232 | tf_op jit(solution)/shard_map/all_gather | solution.py:61
  211.2 14.5 %fusion.18 = bf16[512,2048]{1,0:T(8,128)(2,1)} fusion(bf16[4096,2048]{1,0:T(8,128)(2,1)} %all-gather.5.cloned.1.call-done, bf16[1,512,4096]{2,1,0:T(8,128)(2,1)} %all-gather.3.cloned.1.call-done), kind=kOutput, calls=%fused_computation.26 | convolution fusion | flops 8590983168 | bytes 23068672 | tf_op jit(solution)/shard_map/dot_general | solution.py:62
  225.7 3.9 copy.31
  229.6 11.0 %fusion.39 = (f32[16,512]{1,0:T(8,128)S(1)}, f32[16,512,512]{1,2,0:T(8,128)}) fusion(pred[512]{0:T(512)(128)(4,1)S(1)} %iota_compare_fusion.1, bf16[1,512,16,2,64]{1,4,3,2,0:T(8,128)(2,1)} %bitcast.131, bf16[1,512,16,2,64]{1,4,3,2,0:T(8,128)(2,1)} %bitcast.126), kind=kOutput, calls=%fused_computation.57 | convolution fusion | flops 553648640 | bytes 18907648 | tf_op jit(solution)/shard_map/sub | solution.py:24
  240.7 0.0 copy-start.1
  240.7 6.8 %fusion.8 = bf16[16,512,512]{1,2,0:T(8,128)(2,1)S(1)} fusion(f32[16,512,512]{1,2,0:T(8,128)} %get-tuple-element.9, f32[16,512]{1,0:T(8,128)S(1)} %get-tuple-element.8), kind=kLoop, calls=%fused_computation.12 | loop fusion | flops 8388608 | bytes 25198592 | tf_op jit(solution)/shard_map/convert_element_type | solution.py:26
  247.5 0.0 copy-done.1
  247.5 0.0 copy-start.2
  247.5 3.6 fusion.27
  251.2 0.0 copy-done.2
  251.2 1.5 fusion.23
  252.7 7.8 %multiply_convert_fusion.1 = bf16[16,512,512]{1,2,0:T(8,128)(2,1)S(1)} fusion(f32[16,512]{1,0:T(8,128)S(1)} %fusion.23, f32[16,512,512]{1,2,0:T(8,128)} %get-tuple-element.9, f32[16,512]{1,0:T(8,128)S(1)} %get-tuple-element.8, bf16[1,512,16,2,64]{1,4,3,2,0:T(8,128)(2,1)S(1)} %bitcast.133, bf16[1,512,16,2,64]{1,4,3,2,0:T(8,128)(2,1)S(1)} %bitcast.129, ...), kind=kOutput, calls=%fused_computation.6 | convolution fusion | flops 558366720 | bytes 27329024 | tf_op jit(solution)/shard_map/pihd,pjhd->phij/dot_general | solution.py:28
  260.6 2.6 fusion.26
  263.2 0.0 copy-start.4
  263.2 1.5 fusion.28
  264.7 0.0 copy-done.4
  264.7 1.7 pad_maximum_fusion
  266.4 0.0 copy-start.6
  266.4 0.1 copy.41
  266.5 0.0 copy-start.5
  266.5 1.3 copy-done.5
  267.8 1.5 copy-done.6
  269.3 12.4 %multiply_convert_fusion = bf16[4096,2048]{1,0:T(8,128)(2,1)} fusion(bf16[512,2048]{0,1:T(8,128)(2,1)S(1)} %bitcast.137, bf16[1,512,4096]{2,1,0:T(8,128)(2,1)S(1)} %copy-done.6), kind=kOutput, calls=%fused_computation.1 | convolution fusion | flops 8606711808 | bytes 23068672 | tf_op jit(solution)/shard_map/dot_general | solution.py:78
  281.8 0.0 reduce-scatter.2.cloned.1.call-update
  281.8 14.7 %fusion.9 = bf16[1,1,512,4096]{3,2,1,0:T(8,128)(2,1)} fusion(bf16[512,2048]{0,1:T(8,128)(2,1)} %bitcast.138, bf16[4096,2048]{1,0:T(8,128)(2,1)} %all-gather.5.cloned.1.call-done), kind=kOutput, calls=%fused_computation.14 | convolution fusion | flops 8592031744 | bytes 23068672 | tf_op jit(solution)/shard_map/dot_general | solution.py:89
  296.5 18.9 %copy.42 = bf16[1,1,512,4096]{2,1,0,3:T(2,128)(2,1)} copy(bf16[1,1,512,4096]{3,2,1,0:T(8,128)(2,1)} %fusion.9) | data formatting | bytes 8388608 | tf_op jit(solution)/shard_map/reshape | solution.py:92
  315.4 0.5 broadcast.112
  315.9 28.5 %reduce.11 = bf16[4096,512]{1,0:T(8,128)(2,1)} reduce(bf16[4096,1,1,512]{3,2,1,0:T(2,128)(2,1)} %bitcast.123, bf16[]{:T(256)} %broadcast.112), dimensions={1,2}, to_apply=%bitcast.101.reduce_sub_computation | reduce | bytes 8388610
  344.5 5.9 reshape.260
  350.4 55.6 %all_to_all.4 = bf16[2,2,524288]{2,1,0:T(2,128)(2,1)} all-to-all(bf16[2,2,524288]{2,1,0:T(2,128)(2,1)} %reshape.260), channel_id=1, replica_groups=mesh['dp'=8,'phase'=2,'mp'=2] {'mp'}, dimensions={0} | all-to-all | bytes 8388608 | tf_op jit(solution)/shard_map/all_to_all | solution.py:93
  406.0 7.1 %reshape.261 = bf16[4096,1,1,512]{3,2,1,0:T(2,128)(2,1)} reshape(bf16[2,2,524288]{2,1,0:T(2,128)(2,1)} %all_to_all.4) | data formatting | bytes 8388608
  413.2 7.7 %copy.59 = f32[1,1,512,4096]{2,3,0,1:T(8,128)} copy(bf16[1,1,512,4096]{2,1,0,3:T(2,128)(2,1)} %bitcast.125) | data formatting | bytes 12582912
  420.9 6.9 %reduce_sum.43 = f32[512,2048]{0,1:T(8,128)} reduce(f32[512,2,2048]{0,2,1:T(8,128)} %bitcast.124, f32[]{:T(128)} %constant.3.clone.1), dimensions={1}, to_apply=%region_4.5 | reduce | flops 1048576 | bytes 12582916 | tf_op jit(solution)/shard_map/reduce_sum | solution.py:94
  427.8 5.4 copy.60
  433.2 1.3 collective-permute-start.1
  434.4 127.8 %reduce-scatter.2.cloned.1.call-done = bf16[512,2048]{1,0:T(8,128)(2,1)} async-done(((bf16[4096,2048]{1,0:T(8,128)(2,1)}), bf16[512,2048]{1,0:T(8,128)(2,1)}) %reduce-scatter.2.cloned.1.call-update) | async-done | bytes 2097168 | tf_op jit(solution)/shard_map/reduce_scatter | solution.py:75
  562.2 2.9 slice.28
  565.1 1.3 collective-permute-start.2
  566.4 3.1 copy.45
  569.5 3.9 copy.46
  573.4 0.0 collective-permute-done.1
  573.4 2.8 fusion.13
  576.2 34.9 %psum.15 = f32[2048]{0:T(1024)} all-reduce(f32[2048]{0:T(1024)S(1)} %broadcast_multiply_fusion), channel_id=1, replica_groups=mesh['dp'=8,'phase'=2,'mp'=2] {'dp','phase'}, use_global_device_ids=true, to_apply=%region_7.8 | all-reduce | flops 2048 | bytes 16384 | tf_op jit(solution)/shard_map/psum | solution.py:98
  611.1 0.0 copy-start.3
  611.1 4.4 fusion.22
  615.6 0.0 copy-done.3
  615.6 0.5 convert_element_type.128
  616.1 0.0 collective-permute-done.2
  616.1 3.2 slice_select_fusion
  (4 shorter events, 0.0 us)
Async XLA Ops:
  7.2 74.9 %all-gather.3.cloned.1.call-start = ((), (), s32[]{:S(2)}) async-start(), calls=%async_computation.2 | async-start | bytes 6291456 | tf_op jit(solution)/shard_map/all_gather | solution.py:59
  10.0 14.2 %copy-start = (bf16[1,1,512,2048]{3,2,1,0:T(8,128)(2,1)S(1)}, bf16[1,1,512,2048]{3,2,1,0:T(8,128)(2,1)}, u32[]{:S(2)}) copy-start(bf16[1,1,512,2048]{3,2,1,0:T(8,128)(2,1)} %param.5) | copy-start | bytes 6291460
  18.1 5.2 collective-permute-start
  23.3 187.8 %all-gather.5.cloned.1.call-start = ((), (), s32[]{:S(2)}) async-start(), calls=%async_computation.3 | async-start | bytes 17825792 | tf_op jit(solution)/shard_map/all_gather | solution.py:61
  24.1 538.1 %reduce-scatter.2.cloned.1.call-start = ((), (), s32[]{:S(2)}) async-start(), calls=%async_computation.4 | async-start | bytes 18874368 | tf_op jit(solution)/shard_map/reduce_scatter | solution.py:75
  240.7 6.9 %copy-start.1 = (bf16[1,1,512,2048]{2,3,1,0:T(8,128)(2,1)S(1)}, bf16[1,1,512,2048]{2,3,1,0:T(8,128)(2,1)}, u32[]{:S(2)}) copy-start(bf16[1,1,512,2048]{2,3,1,0:T(8,128)(2,1)} %copy.33) | copy-start | bytes 6291460
  247.5 3.7 copy-start.2
  263.2 1.5 copy-start.4
  266.4 2.9 copy-start.6
  266.5 1.3 copy-start.5
  433.2 140.2 %collective-permute-start.1 = (f32[1,512,2048]{2,1,0:T(8,128)}, f32[1,512,2048]{2,1,0:T(8,128)}, u32[]{:S(2)}, u32[]{:S(2)}) collective-permute-start(f32[1,512,2048]{2,1,0:T(8,128)} %bitcast.136), channel_id=1, source_target_pairs={{2,0},{3,1},{6,4},{7,5},{10,8},{11,9},{14,12},{15,13},{18,16},{19,... | collective-permute-start | bytes 12582920 | tf_op jit(solution)/shard_map/ppermute | solution.py:14
  565.1 51.0 %collective-permute-start.2 = (f32[256,2048]{1,0:T(8,128)}, f32[256,2048]{1,0:T(8,128)}, u32[]{:S(2)}, u32[]{:S(2)}) collective-permute-start(f32[256,2048]{1,0:T(8,128)} %slice.28), channel_id=1, source_target_pairs={{2,0},{3,1},{6,4},{7,5},{10,8},{11,9},{14,12},{15,13},{18,16},{19,... | collective-permute-start | bytes 6291464 | tf_op jit(solution)/shard_map/ppermute | solution.py:14
  611.1 4.4 copy-start.3
Sparse Core Ops, SparseCore 0:
  23.5 58.5 all-gather.2
  84.2 126.8 all-gather.4
  281.9 280.2 reduce-scatter.1
where the time goes:
time: 636 us; the launch traced here: 626 us
  waiting for transfers between devices  314 us (49%)
  blocking collectives  96.5 us (15%)
  matrix products  69.8 us (11%)
  local copies, waits for them, and re-layouts  64.9 us (10%)
  other arithmetic  59.8 us (9%)
  between operations  15.5 us (2%)
    all_gather x1, waiting for transfers between devices, on_device(): whole_weight = lax.all_gather(w_kv, ('dp', 'phase'), axis=0, tiled=True)  129 us
    reduce_scatter x1, waiting for transfers between devices, on_device(): lax.psum_scatter((pair_scale * lax.dot_general(enc_rows, grad_kv, (((0,),...  128 us
    all_to_all x1, blocking collectives, on_device(): lax.all_to_all(partial_enc, 'mp', split_axis=3, concat_axis=0, tiled=True)  55.6 us
    all_gather x1, waiting for transfers between devices, on_device(): enc_full = lax.all_gather(enc_moved, 'mp', axis=2, tiled=True)  54.1 us
    psum x1, blocking collectives, on_device(): d_gain = lax.psum(gain_term, ('dp', 'phase'))  34.9 us
    unnamed x20, local copies, waits for them, and re-layouts  32 us
    unnamed x1, other arithmetic  28.5 us
    reshape x1, local copies, waits for them, and re-layouts, on_device(): partial_enc = partial_enc.reshape(1, pair_dev, length, D)  18.9 us
  transfers between devices with their start and end apart: 6, of which 4 were waited for; matrix products, arithmetic and copies ran while one was open for 19% of the time, Pallas kernels for 0%

commit v1 on v0

--- a/solution.py
+++ b/solution.py
@@ -95,7 +95,7 @@
     grad_enc = shifted(summed, "phase", -1)
     grad_normed = grad_enc * gain_wide
     gain_term = pair_scale * jnp.sum(grad_enc * normed, axis=(0, 1))
-    d_gain = lax.psum(gain_term, ("dp", "phase"))
+    d_gain = lax.psum(lax.psum(gain_term, "phase"), "dp")
     sec_grads = jnp.where(section == 0, grad_normed.astype(bf16), dec_grads)[None]
     return (sec_grads, d_wkv, d_gain)
 

time: 636 us -> 626 us (0.984)
  blocking collectives: 96.5 us -> 86.5 us
    psum x1 -> x2, blocking collectives: 34.9 us -> 24.9 us  [on_device(): d_gain = lax.psum(lax.psum(gain_term, 'phase'), 'dp')]
where the time goes in v1:
time: 626 us; the launch traced here: 616 us
  waiting for transfers between devices  314 us (50%)
  blocking collectives  86.5 us (14%)
  matrix products  69.8 us (11%)
  local copies, waits for them, and re-layouts  64.9 us (10%)
  other arithmetic  59.8 us (10%)
  between operations  15.5 us (2%)
    all_gather x1, waiting for transfers between devices, on_device(): whole_weight = lax.all_gather(w_kv, ('dp', 'phase'), axis=0, tiled=True)  129 us
    reduce_scatter x1, waiting for transfers between devices, on_device(): lax.psum_scatter((pair_scale * lax.dot_general(enc_rows, grad_kv, (((0,),...  128 us
    all_to_all x1, blocking collectives, on_device(): lax.all_to_all(partial_enc, 'mp', split_axis=3, concat_axis=0, tiled=True)  55.6 us
    all_gather x1, waiting for transfers between devices, on_device(): enc_full = lax.all_gather(enc_moved, 'mp', axis=2, tiled=True)  54.1 us
    unnamed x20, local copies, waits for them, and re-layouts  32 us
    unnamed x1, other arithmetic  28.5 us
    psum x2, blocking collectives, on_device(): d_gain = lax.psum(lax.psum(gain_term, 'phase'), 'dp')  24.9 us
    reshape x1, local copies, waits for them, and re-layouts, on_device(): partial_enc = partial_enc.reshape(1, pair_dev, length, D)  18.9 us
  transfers between devices with their start and end apart: 6, of which 4 were waited for; matrix products, arithmetic and copies ran while one was open for 19% of the time, Pallas kernels for 0%

profile of v1, /device:TPU:0, one launch (start us, length us, event | category | flops | bytes accessed | tf_op | source)
XLA Modules:
  0.0 616.0 jit_solution(10454734353962807017)
XLA Ops:
  7.2 0.0 all-gather.3.cloned.1.call-start
  7.2 0.7 convert_element_type.108
  7.9 2.1 fusion.14
  10.0 6.0 psum.21
  16.0 2.1 fusion.12
  18.1 2.7 collective-permute-start
  20.8 2.5 collective-permute-done
  23.3 0.0 all-gather.3.cloned.1.call-update
  23.3 0.0 all-gather.5.cloned.1.call-start
  23.4 0.7 all-gather.5.cloned.1.call-update
  24.1 0.0 reduce-scatter.2.cloned.1.call-start
  24.1 0.0 copy-done
  24.1 2.5 copy.33
  28.0 54.1 %all-gather.3.cloned.1.call-done = bf16[1,512,4096]{2,1,0:T(8,128)(2,1)} async-done(((bf16[1,512,2048]{2,1,0:T(8,128)(2,1)}), bf16[1,512,4096]{2,1,0:T(8,128)(2,1)}) %all-gather.3.cloned.1.call-update) | async-done | bytes 4194320 | tf_op jit(solution)/shard_map/all_gather | solution.py:59
  82.1 129.1 %all-gather.5.cloned.1.call-done = bf16[4096,2048]{1,0:T(8,128)(2,1)} async-done(((bf16[256,2048]{1,0:T(8,128)(2,1)}), bf16[4096,2048]{1,0:T(8,128)(2,1)}) %all-gather.5.cloned.1.call-update) | async-done | bytes 16777232 | tf_op jit(solution)/shard_map/all_gather | solution.py:61
  211.2 14.5 %fusion.18 = bf16[512,2048]{1,0:T(8,128)(2,1)} fusion(bf16[4096,2048]{1,0:T(8,128)(2,1)} %all-gather.5.cloned.1.call-done, bf16[1,512,4096]{2,1,0:T(8,128)(2,1)} %all-gather.3.cloned.1.call-done), kind=kOutput, calls=%fused_computation.26 | convolution fusion | flops 8590983168 | bytes 23068672 | tf_op jit(solution)/shard_map/dot_general | solution.py:62
  225.7 3.9 copy.31
  229.6 11.0 %fusion.39 = (f32[16,512]{1,0:T(8,128)S(1)}, f32[16,512,512]{1,2,0:T(8,128)}) fusion(pred[512]{0:T(512)(128)(4,1)S(1)} %iota_compare_fusion.1, bf16[1,512,16,2,64]{1,4,3,2,0:T(8,128)(2,1)} %bitcast.131, bf16[1,512,16,2,64]{1,4,3,2,0:T(8,128)(2,1)} %bitcast.126), kind=kOutput, calls=%fused_computation.57 | convolution fusion | flops 553648640 | bytes 18907648 | tf_op jit(solution)/shard_map/sub | solution.py:24
  240.7 0.0 copy-start.1
  240.7 6.8 %fusion.8 = bf16[16,512,512]{1,2,0:T(8,128)(2,1)S(1)} fusion(f32[16,512,512]{1,2,0:T(8,128)} %get-tuple-element.9, f32[16,512]{1,0:T(8,128)S(1)} %get-tuple-element.8), kind=kLoop, calls=%fused_computation.12 | loop fusion | flops 8388608 | bytes 25198592 | tf_op jit(solution)/shard_map/convert_element_type | solution.py:26
  247.5 0.0 copy-done.1
  247.5 0.0 copy-start.2
  247.5 3.6 fusion.27
  251.2 0.0 copy-done.2
  251.2 1.5 fusion.23
  252.7 7.8 %multiply_convert_fusion.1 = bf16[16,512,512]{1,2,0:T(8,128)(2,1)S(1)} fusion(f32[16,512]{1,0:T(8,128)S(1)} %fusion.23, f32[16,512,512]{1,2,0:T(8,128)} %get-tuple-element.9, f32[16,512]{1,0:T(8,128)S(1)} %get-tuple-element.8, bf16[1,512,16,2,64]{1,4,3,2,0:T(8,128)(2,1)S(1)} %bitcast.133, bf16[1,512,16,2,64]{1,4,3,2,0:T(8,128)(2,1)S(1)} %bitcast.129, ...), kind=kOutput, calls=%fused_computation.6 | convolution fusion | flops 558366720 | bytes 27329024 | tf_op jit(solution)/shard_map/pihd,pjhd->phij/dot_general | solution.py:28
  260.6 2.6 fusion.26
  263.2 0.0 copy-start.4
  263.2 1.5 fusion.28
  264.7 0.0 copy-done.4
  264.7 1.7 pad_maximum_fusion
  266.4 0.0 copy-start.6
  266.4 0.1 copy.41
  266.5 0.0 copy-start.5
  266.5 1.3 copy-done.5
  267.8 1.5 copy-done.6
  269.3 12.4 %multiply_convert_fusion = bf16[4096,2048]{1,0:T(8,128)(2,1)} fusion(bf16[512,2048]{0,1:T(8,128)(2,1)S(1)} %bitcast.137, bf16[1,512,4096]{2,1,0:T(8,128)(2,1)S(1)} %copy-done.6), kind=kOutput, calls=%fused_computation.1 | convolution fusion | flops 8606711808 | bytes 23068672 | tf_op jit(solution)/shard_map/dot_general | solution.py:78
  281.8 0.0 reduce-scatter.2.cloned.1.call-update
  281.8 14.7 %fusion.9 = bf16[1,1,512,4096]{3,2,1,0:T(8,128)(2,1)} fusion(bf16[512,2048]{0,1:T(8,128)(2,1)} %bitcast.138, bf16[4096,2048]{1,0:T(8,128)(2,1)} %all-gather.5.cloned.1.call-done), kind=kOutput, calls=%fused_computation.14 | convolution fusion | flops 8592031744 | bytes 23068672 | tf_op jit(solution)/shard_map/dot_general | solution.py:89
  296.5 18.9 %copy.42 = bf16[1,1,512,4096]{2,1,0,3:T(2,128)(2,1)} copy(bf16[1,1,512,4096]{3,2,1,0:T(8,128)(2,1)} %fusion.9) | data formatting | bytes 8388608 | tf_op jit(solution)/shard_map/reshape | solution.py:92
  315.4 0.5 broadcast.112
  315.9 28.5 %reduce.11 = bf16[4096,512]{1,0:T(8,128)(2,1)} reduce(bf16[4096,1,1,512]{3,2,1,0:T(2,128)(2,1)} %bitcast.123, bf16[]{:T(256)} %broadcast.112), dimensions={1,2}, to_apply=%bitcast.101.reduce_sub_computation | reduce | bytes 8388610
  344.5 5.9 reshape.260
  350.4 55.6 %all_to_all.4 = bf16[2,2,524288]{2,1,0:T(2,128)(2,1)} all-to-all(bf16[2,2,524288]{2,1,0:T(2,128)(2,1)} %reshape.260), channel_id=1, replica_groups=mesh['dp'=8,'phase'=2,'mp'=2] {'mp'}, dimensions={0} | all-to-all | bytes 8388608 | tf_op jit(solution)/shard_map/all_to_all | solution.py:93
  406.0 7.1 %reshape.261 = bf16[4096,1,1,512]{3,2,1,0:T(2,128)(2,1)} reshape(bf16[2,2,524288]{2,1,0:T(2,128)(2,1)} %all_to_all.4) | data formatting | bytes 8388608
  413.2 7.7 %copy.59 = f32[1,1,512,4096]{2,3,0,1:T(8,128)} copy(bf16[1,1,512,4096]{2,1,0,3:T(2,128)(2,1)} %bitcast.125) | data formatting | bytes 12582912
  420.9 6.9 %reduce_sum.43 = f32[512,2048]{0,1:T(8,128)} reduce(f32[512,2,2048]{0,2,1:T(8,128)} %bitcast.124, f32[]{:T(128)} %constant.3.clone.1), dimensions={1}, to_apply=%region_4.5 | reduce | flops 1048576 | bytes 12582916 | tf_op jit(solution)/shard_map/reduce_sum | solution.py:94
  427.8 5.4 copy.60
  433.2 1.3 collective-permute-start.1
  434.4 127.8 %reduce-scatter.2.cloned.1.call-done = bf16[512,2048]{1,0:T(8,128)(2,1)} async-done(((bf16[4096,2048]{1,0:T(8,128)(2,1)}), bf16[512,2048]{1,0:T(8,128)(2,1)}) %reduce-scatter.2.cloned.1.call-update) | async-done | bytes 2097168 | tf_op jit(solution)/shard_map/reduce_scatter | solution.py:75
  562.2 2.9 slice.28
  565.1 1.3 collective-permute-start.2
  566.4 3.1 copy.45
  569.5 3.9 copy.46
  573.4 0.0 collective-permute-done.1
  573.4 2.8 fusion.13
  576.2 4.6 psum.22
  580.8 20.3 %psum.23 = f32[2048]{0:T(1024)} all-reduce(f32[2048]{0:T(1024)S(1)} %psum.22), channel_id=1, replica_groups=mesh['dp'=8,'phase'=2,'mp'=2] {'dp'}, use_global_device_ids=true, to_apply=%region_8.9 | all-reduce | flops 2048 | bytes 16384 | tf_op jit(solution)/shard_map/psum | solution.py:98
  601.1 0.0 copy-start.3
  601.1 4.4 fusion.22
  605.5 0.0 copy-done.3
  605.5 0.5 convert_element_type.128
  606.0 0.0 collective-permute-done.2
  606.0 3.2 slice_select_fusion
  (5 shorter events, 0.0 us)
Async XLA Ops:
  7.2 74.9 %all-gather.3.cloned.1.call-start = ((), (), s32[]{:S(2)}) async-start(), calls=%async_computation.2 | async-start | bytes 6291456 | tf_op jit(solution)/shard_map/all_gather | solution.py:59
  10.0 14.2 %copy-start = (bf16[1,1,512,2048]{3,2,1,0:T(8,128)(2,1)S(1)}, bf16[1,1,512,2048]{3,2,1,0:T(8,128)(2,1)}, u32[]{:S(2)}) copy-start(bf16[1,1,512,2048]{3,2,1,0:T(8,128)(2,1)} %param.5) | copy-start | bytes 6291460
  18.1 5.2 collective-permute-start
  23.3 187.8 %all-gather.5.cloned.1.call-start = ((), (), s32[]{:S(2)}) async-start(), calls=%async_computation.3 | async-start | bytes 17825792 | tf_op jit(solution)/shard_map/all_gather | solution.py:61
  24.1 538.1 %reduce-scatter.2.cloned.1.call-start = ((), (), s32[]{:S(2)}) async-start(), calls=%async_computation.4 | async-start | bytes 18874368 | tf_op jit(solution)/shard_map/reduce_scatter | solution.py:75
  240.7 6.9 %copy-start.1 = (bf16[1,1,512,2048]{2,3,1,0:T(8,128)(2,1)S(1)}, bf16[1,1,512,2048]{2,3,1,0:T(8,128)(2,1)}, u32[]{:S(2)}) copy-start(bf16[1,1,512,2048]{2,3,1,0:T(8,128)(2,1)} %copy.33) | copy-start | bytes 6291460
  247.5 3.7 copy-start.2
  263.2 1.5 copy-start.4
  266.4 2.9 copy-start.6
  266.5 1.3 copy-start.5
  433.2 140.2 %collective-permute-start.1 = (f32[1,512,2048]{2,1,0:T(8,128)}, f32[1,512,2048]{2,1,0:T(8,128)}, u32[]{:S(2)}, u32[]{:S(2)}) collective-permute-start(f32[1,512,2048]{2,1,0:T(8,128)} %bitcast.136), channel_id=1, source_target_pairs={{2,0},{3,1},{6,4},{7,5},{10,8},{11,9},{14,12},{15,13},{18,16},{19,... | collective-permute-start | bytes 12582920 | tf_op jit(solution)/shard_map/ppermute | solution.py:14
  565.1 41.0 %collective-permute-start.2 = (f32[256,2048]{1,0:T(8,128)}, f32[256,2048]{1,0:T(8,128)}, u32[]{:S(2)}, u32[]{:S(2)}) collective-permute-start(f32[256,2048]{1,0:T(8,128)} %slice.28), channel_id=1, source_target_pairs={{2,0},{3,1},{6,4},{7,5},{10,8},{11,9},{14,12},{15,13},{18,16},{19,... | collective-permute-start | bytes 6291464 | tf_op jit(solution)/shard_map/ppermute | solution.py:14
  601.1 4.4 copy-start.3
Sparse Core Ops, SparseCore 0:
  23.5 58.5 all-gather.2
  84.2 126.8 all-gather.4
  281.9 280.2 reduce-scatter.1
